TPU v7x, 32 devices: a whole 2x2x4 slice. The times are simulated.
32 devices in a mesh: dp: 8 (over y, x, core), shard: 4 (over z).
Axes of the slice: x: 2, y: 2, z: 4, core: 2. Of those that a mesh axis runs over, the one named last changes fastest.
Arguments:
- gradients: bfloat16 [8, 44, 512, 512], P('dp', 'shard'), may hold values from -60 to 60
- owners: int32 [4, 11], P('shard'), may hold values from 0 to 7, as said below
- block_param: int32 [44], replicated, may hold values from 0 to 6, never falling along the last dimension, each value on 1 to 12 neighbouring positions
- left_stat: float32 [16, 4, 512, 512], P('dp', 'shard'), may hold values from -4 to 8, as said below
- right_stat: float32 [16, 4, 512, 512], P('dp', 'shard'), may hold values from -4 to 8, as said below
- moment: float32 [16, 4, 512, 512], P('dp', 'shard'), may hold values from 0.5 to 50
- left_root: bfloat16 [16, 4, 512, 512], P('dp', 'shard'), may hold values from -1 to 3.5, as said below
- right_root: bfloat16 [16, 4, 512, 512], P('dp', 'shard'), may hold values from -1 to 3.5, as said below
Outputs:
- new_left: float32 [16, 4, 512, 512], P('dp', 'shard')
- new_right: float32 [16, 4, 512, 512], P('dp', 'shard')
- new_moment: float32 [16, 4, 512, 512], P('dp', 'shard')
- update: bfloat16 [44, 512, 512], P('shard')
Inputs may be any that keep to these rules, and one draw needn't show every extreme that they name: `owners`: in each row, no value occurs more than 2 times, and some value occurs exactly 2 times. `left_stat`: each slot's matrix is symmetric. `right_stat`: each slot's matrix is symmetric. `left_root`: each slot's matrix is symmetric. `right_root`: each slot's matrix is symmetric.
All inputs are finite; a program needn't handle non-finite values.
Results may differ from a plain program's by a relative error of at most 0.0058.
Values may be sent and summed in bfloat16 or wider, within the bound.
No kernel may reach another device: no remote copies, remote signals or barrier semaphores. Data moves between devices by JAX's collectives and lax.ppermute only.
A program may use at most 192 MiB of HBM per device.

v0:
```python
import jax
import jax.numpy as jnp
from jax import lax
from jax.sharding import PartitionSpec as P

NPARAM = 7
decay_rate = 0.95
tiny_value = 1e-06


def on_device(gradients, owners, block_param, left_stat, right_stat, moment, left_root, right_root):
    replicas = lax.axis_size("dp")
    capacity = left_stat.shape[0]
    blocks = gradients.shape[1]
    block_width = gradients.shape[3]
    device = lax.axis_index("dp")
    column = lax.axis_index("shard")
    owner_row = owners[0]
    counter = jnp.arange(blocks, dtype=jnp.int32)
    same_owner = owner_row[:, None] == owner_row[None, :]
    earlier = counter[None, :] < counter[:, None]
    places = owner_row * capacity + jnp.sum(jnp.where(same_owner & earlier, 1, 0), axis=1).astype(
        jnp.int32
    )
    slot_ids = jnp.arange(replicas * capacity, dtype=jnp.int32)
    matches = places[None, :] == slot_ids[:, None]
    source = jnp.min(jnp.where(matches, counter[None, :], blocks), axis=1)
    partials = gradients[0].astype(jnp.float32)
    row_share = lax.psum_scatter(partials, "dp", scatter_dimension=1, tiled=True)
    share_padded = jnp.concatenate(
        [row_share, jnp.zeros((1,) + row_share.shape[1:], jnp.float32)], axis=0
    )
    outgoing = jnp.take(share_padded, source, axis=0).reshape(
        replicas, capacity, block_width // replicas, block_width
    )
    arrived = lax.all_to_all(outgoing, "dp", split_axis=0, concat_axis=2, tiled=True)
    summed = arrived[0]
    left_gram = jnp.einsum("cij,ckj->cik", summed, summed, precision=lax.Precision.HIGHEST)
    right_gram = jnp.einsum("cji,cjk->cik", summed, summed, precision=lax.Precision.HIGHEST)
    new_left = decay_rate * left_stat + (1.0 - decay_rate) * left_gram[:, None]
    new_right = decay_rate * right_stat + (1.0 - decay_rate) * right_gram[:, None]
    new_moment = decay_rate * moment + (1.0 - decay_rate) * (summed * summed)[:, None]
    adam_step = summed / (jnp.sqrt(new_moment[:, 0]) + tiny_value)
    left_half = jnp.einsum(
        "cij,cjk->cik",
        left_root[:, 0],
        summed.astype(jnp.bfloat16),
        preferred_element_type=jnp.float32,
    ).astype(jnp.bfloat16)
    direction = jnp.einsum(
        "cij,cjk->cik", left_half, right_root[:, 0], preferred_element_type=jnp.float32
    )
    my_slots = lax.dynamic_slice_in_dim(matches, device * capacity, capacity, 0)
    local_params = lax.dynamic_slice_in_dim(block_param, column * blocks, blocks, 0)
    slot_param = jnp.sum(jnp.where(my_slots, local_params[None, :], 0), axis=1)
    is_live = jnp.any(my_slots, axis=1)
    param_ids = jnp.arange(NPARAM, dtype=jnp.int32)
    member = (slot_param[:, None] == param_ids[None, :]) & is_live[:, None]
    adam_squares = jnp.sum(adam_step * adam_step, axis=(1, 2))
    direction_squares = jnp.sum(direction * direction, axis=(1, 2))
    adam_local = jnp.sum(jnp.where(member, adam_squares[:, None], 0.0), axis=0)
    direction_local = jnp.sum(jnp.where(member, direction_squares[:, None], 0.0), axis=0)
    adam_norm, direction_norm = lax.psum((adam_local, direction_local), ("dp", "shard"))
    graft_ratio = jnp.sqrt((adam_norm + tiny_value) / (direction_norm + tiny_value))
    slot_ratio = jnp.sum(jnp.where(member, graft_ratio[None, :], 0.0), axis=1)
    slot_update = (slot_ratio[:, None, None] * direction).astype(jnp.bfloat16)
    gathered = lax.all_gather(slot_update, "dp", axis=0, tiled=True)
    update = jnp.take(gathered, places, axis=0)
    return (new_left, new_right, new_moment, update)


def solution(mesh):
    return jax.shard_map(
        on_device,
        mesh=mesh,
        in_specs=(
            P("dp", "shard", None, None),
            P("shard", None),
            P(),
            P("dp", "shard", None, None),
            P("dp", "shard", None, None),
            P("dp", "shard", None, None),
            P("dp", "shard", None, None),
            P("dp", "shard", None, None),
        ),
        out_specs=(
            P("dp", "shard", None, None),
            P("dp", "shard", None, None),
            P("dp", "shard", None, None),
            P("shard", None, None),
        ),
        check_vma=False,
    )
```

profile of v0, /device:TPU:0, one launch (start us, length us, event | category | flops | bytes accessed | tf_op | source)
XLA Modules:
  0.0 273.2 jit_solution(2395701479978908789)
XLA Ops:
  7.2 8.7 %bitcast_convert_fusion = f32[11,512,512]{2,1,0:T(8,128)} fusion(bf16[1,11,512,512]{3,2,1,0:T(8,128)(2,1)} %param.8), kind=kLoop, calls=%fused_computation.2 | loop fusion | flops 2883584 | bytes 17301504 | tf_op jit(solution)/shard_map/convert_element_type | solution.py:28
  15.9 0.6 copy-done.6
  17.0 88.7 %reduce-scatter.2.cloned.1.call-done = f32[11,64,512]{2,1,0:T(8,128)} async-done(((f32[11,512,512]{2,1,0:T(8,128)}), f32[11,64,512]{2,1,0:T(8,128)}) %reduce-scatter.2.cloned.1.call-update) | async-done | bytes 1441808 | tf_op jit(solution)/shard_map/reduce_scatter | solution.py:29
  105.6 1.5 concatenate.3
  107.2 2.0 gather_fusion
  109.2 3.3 %broadcast_select_fusion.1 = f32[8,2,64,512]{3,2,1,0:T(8,128)} fusion(f32[8,2,64,512]{3,2,1,0:T(8,128)} %bitcast.79, pred[8,2]{1,0:T(8,128)(4,1)S(1)} %compare_and_fusion), kind=kLoop, calls=%fused_computation.24 | loop fusion | flops 524288 | bytes 4194320 | tf_op jit(solution)/shard_map/jit(_take)/select_n | solution.py:33
  112.5 3.7 %all-to-all-start = ((f32[8,2,64,512]{3,2,1,0:T(8,128)}), f32[8,2,64,512]{3,2,1,0:T(8,128)S(1)}, u32[]{:S(2)}, u32[]{:S(2)}) async-start(f32[8,2,64,512]{3,2,1,0:T(8,128)} %broadcast_select_fusion.1), calls=%async_computation.1 | async-start | bytes 4194304 | tf_op jit(solution)/shard_map/all_to_all | solution.py:36
  116.6 26.2 %all-to-all-done = f32[8,2,64,512]{3,2,1,0:T(8,128)S(1)} async-done(((f32[8,2,64,512]{3,2,1,0:T(8,128)}), f32[8,2,64,512]{3,2,1,0:T(8,128)S(1)}, u32[]{:S(2)}, u32[]{:S(2)}) %all-to-all-start) | async-done | bytes 2097184 | tf_op jit(solution)/shard_map/all_to_all | solution.py:36
  142.8 0.3 multiply_multiply_fusion
  143.1 1.1 copy-done.2
  144.1 0.2 copy.47
  144.3 2.0 copy.43
  146.3 0.2 copy-done.3
  146.6 2.8 %sqrt_add_fusion = (f32[2,1,512,512]{3,2,0,1:T(8,128)}, f32[2,1,512,512]{3,2,0,1:T(8,128)}) fusion(f32[1,2,8,64,512]{4,3,2,1,0:T(8,128)S(1)} %copy.47, f32[2,1,512,512]{3,2,1,0:T(8,128)S(1)} %copy-done.3), kind=kLoop, calls=%fused_computation.16 | loop fusion | flops 1572864 | bytes 8388608 | tf_op jit(solution)/shard_map/add | solution.py:43
  149.3 4.0 %multiply_reduce_fusion = (f32[2]{0:T(128)S(1)}, f32[2,512,512]{2,1,0:T(8,128)}) fusion(bf16[2,1,512,512]{3,2,1,0:T(8,128)(2,1)S(1)} %copy-done, bf16[2,1,512,512]{3,2,1,0:T(8,128)(2,1)} %param.14, f32[2,512,512]{2,1,0:T(8,128)S(1)} %bitcast.75), kind=kOutput, calls=%fused_computation.15 | convolution fusion | flops 1075838976 | bytes 6291464 | tf_op jit(solution)/shard_map/cij,cjk->cik/dot_general | solution.py:50
  153.3 2.7 fusion.3
  156.1 39.5 %all-reduce.1 = (f32[7]{0:T(128)S(1)}, f32[7]{0:T(128)S(1)}) all-reduce(f32[7]{0:T(128)S(1)} %get-tuple-element.21, f32[7]{0:T(128)S(1)} %get-tuple-element.20), channel_id=1, replica_groups=mesh['dp'=8,'shard'=4] {'dp','shard'}, use_global_device_ids=true, to_apply=%region_10.11 | all-reduce | flops 14 | bytes 112 | tf_op jit(solution)/shard_map/psum | solution.py:63
  195.5 0.2 select_reduce_fusion.2
  195.7 3.0 %multiply_convert_fusion = bf16[2,512,512]{2,1,0:T(8,128)(2,1)} fusion(f32[2,512,512]{2,1,0:T(8,128)} %get-tuple-element.27, f32[2]{0:T(128)S(1)} %select_reduce_fusion.2), kind=kLoop, calls=%fused_computation.14 | loop fusion | flops 1048576 | bytes 3145736 | tf_op jit(solution)/shard_map/convert_element_type | solution.py:66
  198.8 6.1 %fusion = f32[2,1,512,512]{3,2,1,0:T(8,128)} fusion(f32[2,1,512,512]{3,2,1,0:T(8,128)} %param.12, f32[2,512,512]{2,1,0:T(8,128)S(1)} %bitcast.76), kind=kOutput, calls=%fused_computation.7 | convolution fusion | flops 3222798336 | bytes 6291456 | tf_op jit(solution)/shard_map/cji,cjk->cik/dot_general | solution.py:39
  204.9 5.0 %fusion.1 = f32[2,1,512,512]{3,2,1,0:T(8,128)} fusion(f32[2,1,512,512]{3,2,1,0:T(8,128)S(1)} %copy-done.4, f32[2,512,512]{2,1,0:T(8,128)S(1)} %bitcast.77), kind=kOutput, calls=%fused_computation.10 | convolution fusion | flops 3222798336 | bytes 6291456 | tf_op jit(solution)/shard_map/cij,ckj->cik/dot_general | solution.py:38
  209.9 43.1 %all-gather.2.cloned.1.call-done = bf16[16,512,512]{2,1,0:T(8,128)(2,1)} async-done(((bf16[2,512,512]{2,1,0:T(8,128)(2,1)}), bf16[16,512,512]{2,1,0:T(8,128)(2,1)}) %all-gather.2.cloned.1.call-update) | async-done | bytes 8388624 | tf_op jit(solution)/shard_map/all_gather | solution.py:67
  253.0 7.4 %gather_fusion.1 = bf16[11,512,512]{2,1,0:T(8,128)(2,1)} fusion(bf16[16,512,512]{2,1,0:T(8,128)(2,1)} %all-gather.2.cloned.1.call-done, s32[1024]{0:T(1024)S(1)} %pad_clamp_fusion), kind=kCustom, calls=%fused_computation.1 | custom fusion | bytes 11534380 | tf_op jit(solution)/shard_map/jit(_take)/gather | solution.py:68
  260.5 5.9 %broadcast_select_fusion = bf16[11,512,512]{2,1,0:T(8,128)(2,1)} fusion(bf16[11,512,512]{2,1,0:T(8,128)(2,1)} %gather_fusion.1, pred[11]{0:T(512)(128)(4,1)S(1)} %compare_and_fusion.2), kind=kLoop, calls=%fused_computation.3 | loop fusion | flops 2883584 | bytes 11534347 | tf_op jit(solution)/shard_map/jit(_take)/select_n | solution.py:68
  (31 shorter events, 1.0 us)
Async XLA Ops:
  7.2 142.2 %copy-start = (bf16[2,1,512,512]{3,2,1,0:T(8,128)(2,1)S(1)}, bf16[2,1,512,512]{3,2,1,0:T(8,128)(2,1)}, u32[]{:S(2)}) copy-start(bf16[2,1,512,512]{3,2,1,0:T(8,128)(2,1)} %param.15) | copy-start | bytes 3145732
  7.2 98.5 %reduce-scatter.2.cloned.1.call-start = ((), (), s32[]{:S(2)}) async-start(), calls=%async_computation.2 | async-start | bytes 12976128 | tf_op jit(solution)/shard_map/reduce_scatter | solution.py:29
  15.9 0.7 copy-start.6
  112.5 3.8 %copy-start.5 = (s32[44]{0:T(128)S(1)}, s32[44]{0:T(128)}, u32[]{:S(2)}) copy-start(s32[44]{0:T(128)} %param.10) | copy-start | bytes 532
  112.5 30.3 %all-to-all-start = ((f32[8,2,64,512]{3,2,1,0:T(8,128)}), f32[8,2,64,512]{3,2,1,0:T(8,128)S(1)}, u32[]{:S(2)}, u32[]{:S(2)}) async-start(f32[8,2,64,512]{3,2,1,0:T(8,128)} %broadcast_select_fusion.1), calls=%async_computation.1 | async-start | bytes 4194304 | tf_op jit(solution)/shard_map/all_to_all | solution.py:36
  116.2 136.8 %all-gather.2.cloned.1.call-start = ((), (), s32[]{:S(2)}) async-start(), calls=%async_computation.3 | async-start | bytes 9437184 | tf_op jit(solution)/shard_map/all_gather | solution.py:67
  142.8 1.3 copy-start.2
  144.3 2.2 copy-start.3
  198.8 6.2 %copy-start.4 = (f32[2,1,512,512]{3,2,1,0:T(8,128)S(1)}, f32[2,1,512,512]{3,2,1,0:T(8,128)}, u32[]{:S(2)}) copy-start(f32[2,1,512,512]{3,2,1,0:T(8,128)} %param.11) | copy-start | bytes 6291460
  260.5 5.9 %copy-start.1 = (bf16[2,1,512,512]{3,2,1,0:T(8,128)(2,1)S(1)}, bf16[2,1,512,512]{3,2,1,0:T(8,128)(2,1)}, u32[]{:S(2)}) copy-start(bf16[2,1,512,512]{3,2,1,0:T(8,128)(2,1)} %param.15) | copy-start | bytes 3145732
Sparse Core Ops, SparseCore 0:
  16.0 89.5 reduce-scatter.1
  198.9 54.1 all-gather.1
where the time goes:
time: 274 us; the launch traced here: 273 us
  waiting for transfers between devices  158 us (58%)
  blocking collectives  39.5 us (14%)
  other arithmetic  27.4 us (10%)
  local copies, waits for them, and re-layouts  15.3 us (6%)
  matrix products  15.1 us (6%)
  between operations  14.2 us (5%)
  starting transfers between devices  3.82 us (1%)
    reduce_scatter x1, waiting for transfers between devices, on_device(): lax.psum_scatter(partials, 'dp', scatter_dimension=1, tiled=True)  88.7 us
    all_gather x1, waiting for transfers between devices, on_device(): gathered = lax.all_gather(slot_update, 'dp', axis=0, tiled=True)  43.1 us
    psum x1, blocking collectives, on_device(): lax.psum((adam_local, direction_local), ('dp', 'shard'))  39.5 us
    all_to_all x1, waiting for transfers between devices, on_device(): lax.all_to_all(outgoing, 'dp', split_axis=0, concat_axis=2, tiled=True)  26.2 us
    convert_element_type x1, other arithmetic, on_device(): partials = gradients[0].astype(jnp.float32)  8.67 us
    gather x1, local copies, waits for them, and re-layouts, on_device(): update = jnp.take(gathered, places, axis=0)  7.44 us
    dot_general x1, matrix products, on_device(): jnp.einsum('cji,cjk->cik', summed, summed, precision=lax.Precision.HIGHEST)  6.14 us
    select_n x2, other arithmetic, on_device(): update = jnp.take(gathered, places, axis=0)  5.87 us
  transfers between devices with their start and end apart: 3, of which 3 were waited for; matrix products, arithmetic and copies ran while one was open for 4% of the time, Pallas kernels for 0%

commit v1 on v0

--- a/solution.py
+++ b/solution.py
@@ -60,7 +60,7 @@
     direction_squares = jnp.sum(direction * direction, axis=(1, 2))
     adam_local = jnp.sum(jnp.where(member, adam_squares[:, None], 0.0), axis=0)
     direction_local = jnp.sum(jnp.where(member, direction_squares[:, None], 0.0), axis=0)
-    adam_norm, direction_norm = lax.psum((adam_local, direction_local), ("dp", "shard"))
+    adam_norm, direction_norm = lax.psum(lax.psum((adam_local, direction_local), "dp"), "shard")
     graft_ratio = jnp.sqrt((adam_norm + tiny_value) / (direction_norm + tiny_value))
     slot_ratio = jnp.sum(jnp.where(member, graft_ratio[None, :], 0.0), axis=1)
     slot_update = (slot_ratio[:, None, None] * direction).astype(jnp.bfloat16)

time: 274 us -> 255 us (0.931)
  blocking collectives: 39.5 us -> 23.7 us
  waiting for transfers between devices: 158 us -> 155 us
    psum x1 -> x2, blocking collectives: 39.5 us -> 23.7 us  [the longest x1 11.9 us: on_device(): lax.psum(lax.psum((adam_local, direction_local), 'dp'), 'shard')]
  transfers between devices with their start and end apart: 3 -> 3, of which waited for: 3 -> 3; matrix products, arithmetic and copies ran while one was open for 4% -> 5% of each run, Pallas kernels for 0% -> 0%
where the time goes in v1:
time: 255 us
  waiting for transfers between devices  155 us (61%)
  other arithmetic  27.4 us (11%)
  blocking collectives  23.7 us (9%)
  local copies, waits for them, and re-layouts  15.3 us (6%)
  matrix products  15.1 us (6%)
  between operations  14.2 us (6%)
  starting transfers between devices  3.82 us (1%)
    reduce_scatter x1, waiting for transfers between devices, on_device(): lax.psum_scatter(partials, 'dp', scatter_dimension=1, tiled=True)  88.7 us
    all_gather x1, waiting for transfers between devices, on_device(): gathered = lax.all_gather(slot_update, 'dp', axis=0, tiled=True)  40.6 us
    all_to_all x1, waiting for transfers between devices, on_device(): lax.all_to_all(outgoing, 'dp', split_axis=0, concat_axis=2, tiled=True)  26.2 us
    psum x1, blocking collectives, on_device(): lax.psum(lax.psum((adam_local, direction_local), 'dp'), 'shard')  11.9 us
    psum x1, blocking collectives, on_device(): lax.psum((adam_local, direction_local), 'dp')  11.8 us
    convert_element_type x1, other arithmetic, on_device(): partials = gradients[0].astype(jnp.float32)  8.67 us
    gather x1, local copies, waits for them, and re-layouts, on_device(): update = jnp.take(gathered, places, axis=0)  7.44 us
    dot_general x1, matrix products, on_device(): jnp.einsum('cji,cjk->cik', summed, summed, precision=lax.Precision.HIGHEST)  6.14 us
  transfers between devices with their start and end apart: 3, of which 3 were waited for; matrix products, arithmetic and copies ran while one was open for 5% of the time, Pallas kernels for 0%

profile of v1, /device:TPU:0, one launch (start us, length us, event | category | flops | bytes accessed | tf_op | source)
XLA Modules:
  0.0 254.9 jit_solution(1108206770472459608)
XLA Ops:
  7.2 8.7 %bitcast_convert_fusion = f32[11,512,512]{2,1,0:T(8,128)} fusion(bf16[1,11,512,512]{3,2,1,0:T(8,128)(2,1)} %param.8), kind=kLoop, calls=%fused_computation.2 | loop fusion | flops 2883584 | bytes 17301504 | tf_op jit(solution)/shard_map/convert_element_type | solution.py:28
  15.9 0.6 copy-done.6
  17.0 88.7 %reduce-scatter.2.cloned.1.call-done = f32[11,64,512]{2,1,0:T(8,128)} async-done(((f32[11,512,512]{2,1,0:T(8,128)}), f32[11,64,512]{2,1,0:T(8,128)}) %reduce-scatter.2.cloned.1.call-update) | async-done | bytes 1441808 | tf_op jit(solution)/shard_map/reduce_scatter | solution.py:29
  105.6 1.5 concatenate.3
  107.2 2.0 gather_fusion
  109.2 3.3 %broadcast_select_fusion.1 = f32[8,2,64,512]{3,2,1,0:T(8,128)} fusion(f32[8,2,64,512]{3,2,1,0:T(8,128)} %bitcast.79, pred[8,2]{1,0:T(8,128)(4,1)S(1)} %compare_and_fusion), kind=kLoop, calls=%fused_computation.24 | loop fusion | flops 524288 | bytes 4194320 | tf_op jit(solution)/shard_map/jit(_take)/select_n | solution.py:33
  112.5 3.7 %all-to-all-start = ((f32[8,2,64,512]{3,2,1,0:T(8,128)}), f32[8,2,64,512]{3,2,1,0:T(8,128)S(1)}, u32[]{:S(2)}, u32[]{:S(2)}) async-start(f32[8,2,64,512]{3,2,1,0:T(8,128)} %broadcast_select_fusion.1), calls=%async_computation.1 | async-start | bytes 4194304 | tf_op jit(solution)/shard_map/all_to_all | solution.py:36
  116.6 26.2 %all-to-all-done = f32[8,2,64,512]{3,2,1,0:T(8,128)S(1)} async-done(((f32[8,2,64,512]{3,2,1,0:T(8,128)}), f32[8,2,64,512]{3,2,1,0:T(8,128)S(1)}, u32[]{:S(2)}, u32[]{:S(2)}) %all-to-all-start) | async-done | bytes 2097184 | tf_op jit(solution)/shard_map/all_to_all | solution.py:36
  142.8 0.3 multiply_multiply_fusion
  143.1 1.1 copy-done.2
  144.1 0.2 copy.47
  144.3 2.0 copy.43
  146.3 0.2 copy-done.3
  146.6 2.8 %sqrt_add_fusion = (f32[2,1,512,512]{3,2,0,1:T(8,128)}, f32[2,1,512,512]{3,2,0,1:T(8,128)}) fusion(f32[1,2,8,64,512]{4,3,2,1,0:T(8,128)S(1)} %copy.47, f32[2,1,512,512]{3,2,1,0:T(8,128)S(1)} %copy-done.3), kind=kLoop, calls=%fused_computation.16 | loop fusion | flops 1572864 | bytes 8388608 | tf_op jit(solution)/shard_map/add | solution.py:43
  149.3 4.0 %multiply_reduce_fusion = (f32[2]{0:T(128)S(1)}, f32[2,512,512]{2,1,0:T(8,128)}) fusion(bf16[2,1,512,512]{3,2,1,0:T(8,128)(2,1)S(1)} %copy-done, bf16[2,1,512,512]{3,2,1,0:T(8,128)(2,1)} %param.14, f32[2,512,512]{2,1,0:T(8,128)S(1)} %bitcast.75), kind=kOutput, calls=%fused_computation.15 | convolution fusion | flops 1075838976 | bytes 6291464 | tf_op jit(solution)/shard_map/cij,cjk->cik/dot_general | solution.py:50
  153.3 2.7 %fusion.3 = f32[2]{0:T(128)S(1)} fusion(f32[1,2,8,64,512]{4,3,2,1,0:T(8,128)} %bitcast.80, f32[8,2,64,512]{3,2,1,0:T(8,128)} %copy-done.2), kind=kLoop, calls=%fused_computation.18 | loop fusion | flops 1572862 | bytes 4194312 | tf_op jit(solution)/shard_map/reduce_sum | solution.py:59
  156.1 11.8 %all-reduce.1 = (f32[7]{0:T(128)S(1)}, f32[7]{0:T(128)S(1)}) all-reduce(f32[7]{0:T(128)S(1)} %get-tuple-element.21, f32[7]{0:T(128)S(1)} %get-tuple-element.20), channel_id=1, replica_groups=mesh['dp'=8,'shard'=4] {'dp'}, use_global_device_ids=true, to_apply=%region_11.12 | all-reduce | flops 14 | bytes 112 | tf_op jit(solution)/shard_map/psum | solution.py:63
  167.9 11.9 %all-reduce.2 = (f32[7]{0:T(128)S(1)}, f32[7]{0:T(128)S(1)}) all-reduce(f32[7]{0:T(128)S(1)} %get-tuple-element.22, f32[7]{0:T(128)S(1)} %get-tuple-element.23), channel_id=1, replica_groups=mesh['dp'=8,'shard'=4] {'shard'}, use_global_device_ids=true, to_apply=%region_12.13 | all-reduce | flops 14 | bytes 112 | tf_op jit(solution)/shard_map/psum | solution.py:63
  179.9 3.0 %multiply_convert_fusion = bf16[2,512,512]{2,1,0:T(8,128)(2,1)} fusion(f32[2,512,512]{2,1,0:T(8,128)} %get-tuple-element.29, f32[2]{0:T(128)S(1)} %select_reduce_fusion.2), kind=kLoop, calls=%fused_computation.14 | loop fusion | flops 1048576 | bytes 3145736 | tf_op jit(solution)/shard_map/convert_element_type | solution.py:66
  183.0 6.1 %fusion = f32[2,1,512,512]{3,2,1,0:T(8,128)} fusion(f32[2,1,512,512]{3,2,1,0:T(8,128)} %param.12, f32[2,512,512]{2,1,0:T(8,128)S(1)} %bitcast.76), kind=kOutput, calls=%fused_computation.7 | convolution fusion | flops 3222798336 | bytes 6291456 | tf_op jit(solution)/shard_map/cji,cjk->cik/dot_general | solution.py:39
  189.1 5.0 %fusion.1 = f32[2,1,512,512]{3,2,1,0:T(8,128)} fusion(f32[2,1,512,512]{3,2,1,0:T(8,128)S(1)} %copy-done.4, f32[2,512,512]{2,1,0:T(8,128)S(1)} %bitcast.77), kind=kOutput, calls=%fused_computation.10 | convolution fusion | flops 3222798336 | bytes 6291456 | tf_op jit(solution)/shard_map/cij,ckj->cik/dot_general | solution.py:38
  194.1 40.6 %all-gather.2.cloned.1.call-done = bf16[16,512,512]{2,1,0:T(8,128)(2,1)} async-done(((bf16[2,512,512]{2,1,0:T(8,128)(2,1)}), bf16[16,512,512]{2,1,0:T(8,128)(2,1)}) %all-gather.2.cloned.1.call-update) | async-done | bytes 8388624 | tf_op jit(solution)/shard_map/all_gather | solution.py:67
  234.7 7.4 %gather_fusion.1 = bf16[11,512,512]{2,1,0:T(8,128)(2,1)} fusion(bf16[16,512,512]{2,1,0:T(8,128)(2,1)} %all-gather.2.cloned.1.call-done, s32[1024]{0:T(1024)S(1)} %pad_clamp_fusion), kind=kCustom, calls=%fused_computation.1 | custom fusion | bytes 11534380 | tf_op jit(solution)/shard_map/jit(_take)/gather | solution.py:68
  242.2 5.9 %broadcast_select_fusion = bf16[11,512,512]{2,1,0:T(8,128)(2,1)} fusion(bf16[11,512,512]{2,1,0:T(8,128)(2,1)} %gather_fusion.1, pred[11]{0:T(512)(128)(4,1)S(1)} %compare_and_fusion.2), kind=kLoop, calls=%fused_computation.3 | loop fusion | flops 2883584 | bytes 11534347 | tf_op jit(solution)/shard_map/jit(_take)/select_n | solution.py:68
  (32 shorter events, 1.2 us)
Async XLA Ops:
  7.2 142.2 %copy-start = (bf16[2,1,512,512]{3,2,1,0:T(8,128)(2,1)S(1)}, bf16[2,1,512,512]{3,2,1,0:T(8,128)(2,1)}, u32[]{:S(2)}) copy-start(bf16[2,1,512,512]{3,2,1,0:T(8,128)(2,1)} %param.15) | copy-start | bytes 3145732
  7.2 98.5 %reduce-scatter.2.cloned.1.call-start = ((), (), s32[]{:S(2)}) async-start(), calls=%async_computation.2 | async-start | bytes 12976128 | tf_op jit(solution)/shard_map/reduce_scatter | solution.py:29
  15.9 0.7 copy-start.6
  112.5 3.8 %copy-start.5 = (s32[44]{0:T(128)S(1)}, s32[44]{0:T(128)}, u32[]{:S(2)}) copy-start(s32[44]{0:T(128)} %param.10) | copy-start | bytes 532
  112.5 30.3 %all-to-all-start = ((f32[8,2,64,512]{3,2,1,0:T(8,128)}), f32[8,2,64,512]{3,2,1,0:T(8,128)S(1)}, u32[]{:S(2)}, u32[]{:S(2)}) async-start(f32[8,2,64,512]{3,2,1,0:T(8,128)} %broadcast_select_fusion.1), calls=%async_computation.1 | async-start | bytes 4194304 | tf_op jit(solution)/shard_map/all_to_all | solution.py:36
  116.2 118.5 %all-gather.2.cloned.1.call-start = ((), (), s32[]{:S(2)}) async-start(), calls=%async_computation.3 | async-start | bytes 9437184 | tf_op jit(solution)/shard_map/all_gather | solution.py:67
  142.8 1.3 copy-start.2
  144.3 2.2 copy-start.3
  183.0 6.2 %copy-start.4 = (f32[2,1,512,512]{3,2,1,0:T(8,128)S(1)}, f32[2,1,512,512]{3,2,1,0:T(8,128)}, u32[]{:S(2)}) copy-start(f32[2,1,512,512]{3,2,1,0:T(8,128)} %param.11) | copy-start | bytes 6291460
  242.2 5.9 %copy-start.1 = (bf16[2,1,512,512]{3,2,1,0:T(8,128)(2,1)S(1)}, bf16[2,1,512,512]{3,2,1,0:T(8,128)(2,1)}, u32[]{:S(2)}) copy-start(bf16[2,1,512,512]{3,2,1,0:T(8,128)(2,1)} %param.15) | copy-start | bytes 3145732
Sparse Core Ops, SparseCore 0:
  16.0 89.5 reduce-scatter.1
  183.1 51.6 all-gather.1
